TPU v7x, 256 devices: a whole 4x4x8 slice. The times are simulated.
256 devices in a mesh: ex: 32 (over z, y_hi, core), grp: 8 (over y_lo, x).
Axes of the slice: x: 4, y: 4 (y_hi: 2, y_lo: 2; y = y_hi * 2 + y_lo), z: 8, core: 2. Of those that a mesh axis runs over, the one named last changes fastest.
Arguments:
- queries: bfloat16 [8192, 65536], P('ex', 'grp'), may hold values from -6 to 6
- inv_in: bfloat16 [16, 64, 64], P('grp'), as said below
- inv_out: bfloat16 [16, 64, 64], P('grp'), as said below
- store: bfloat16 [16384, 65536], P('ex', 'grp'), may hold values from -0.0234375 to 0.0234375
- listed: int32 [256, 24], P('ex'), may hold values from 0 to 1, as said below
Outputs:
- scores: float32 [3, 8192, 512], P(None, ('ex', 'grp'))
Inputs may be any that keep to these rules, and one draw needn't show every extreme that they name: Entries are 0 or 1; every query block lists column 0 and column 23, the other numbers listed differ from block to block and from ex block to ex block, and some query block lists all 24. `inv_in`: each matrix is symmetric and positive definite. `inv_out`: each matrix is symmetric and positive definite.
All inputs are finite; a program needn't handle non-finite values.
Results may differ from a plain program's by a relative error of at most 0.0041.
Values may be sent and summed in bfloat16 or wider, within the bound.
A program may use at most 64 MiB of HBM per device.

v0:
```python
import jax
import jax.numpy as jnp
from jax import lax
from jax.sharding import PartitionSpec as P

QB = 32
SUB = 64


def shifted(value, axis, steps):
    count = lax.axis_size(axis)
    pairs = [(source, (source + steps) % count) for source in range(count)]
    return lax.ppermute(value, axis, pairs)


def precondition(queries, inv_in, inv_out):
    count = queries.shape[0]
    modules = inv_in.shape[0]
    side = inv_in.shape[1]
    query_part = queries.reshape(count, modules, side, side)
    left = jnp.einsum(
        "mab,qmbc->qmac", inv_in, query_part, preferred_element_type=jnp.float32
    ).astype(jnp.bfloat16)
    ready = jnp.einsum("qmac,mcd->qmad", left, inv_out, preferred_element_type=jnp.float32)
    return ready.reshape(count, modules * side * side).astype(jnp.bfloat16)


def widen(listed_rows, first, count):
    piece = lax.slice_in_dim(listed_rows, first, first + count, axis=1).astype(jnp.float32)
    blocks = piece.shape[0]
    full = jnp.broadcast_to(piece[:, None, :, None], (blocks, QB, count, SUB))
    return full.reshape(blocks * QB, count * SUB)


def score(ready, slab, listed_rows, window):
    blocks = slab.shape[0] // SUB
    part = lax.dot_general(
        ready, slab, (((1,), (1,)), ((), ())), preferred_element_type=jnp.float32
    )
    return part * widen(listed_rows, window * blocks, blocks)


def body(queries, inv_in, inv_out, store, listed):
    ready = precondition(queries, inv_in, inv_out)
    own_part = score(ready, store, listed, 1)
    lower_items = shifted((ready, listed), "ex", 1)
    upper_items = shifted((ready, listed), "ex", -1)
    visit_upper = score(upper_items[0], store, upper_items[1], 0)
    visit_lower = score(lower_items[0], store, lower_items[1], 2)
    upper_back = shifted(visit_upper, "ex", 1)
    lower_back = shifted(visit_lower, "ex", -1)
    stacked = jnp.stack([upper_back, own_part, lower_back])
    summed = lax.psum_scatter(stacked, "grp", scatter_dimension=1, tiled=True)
    return summed


def solution(mesh):
    in_specs = (
        P("ex", "grp"),
        P("grp", None, None),
        P("grp", None, None),
        P("ex", "grp"),
        P("ex", None),
    )
    out_specs = P(None, ("ex", "grp"), None)
    return jax.shard_map(body, mesh=mesh, in_specs=in_specs, out_specs=out_specs, check_vma=False)
```

profile of v0, /device:TPU:32, one launch (start us, length us, event | category | flops | bytes accessed | tf_op | source)
XLA Modules:
  0.0 204.3 jit_solution(9924358023960705137)
XLA Ops:
  6.5 6.4 %copy.7 = bf16[256,8192]{0,1:T(8,128)(2,1)} copy(bf16[256,8192]{1,0:T(8,128)(2,1)} %param.5) | data formatting | bytes 8388608 | tf_op args[0]
  12.9 5.5 %fusion.3 = bf16[2,256,64,64]{1,3,2,0:T(8,128)(2,1)S(1)} fusion(bf16[256,2,64,64]{0,3,2,1:T(8,128)(2,1)} %bitcast.35, bf16[2,64,64]{2,1,0:T(8,128)(2,1)S(1)} %copy-done), kind=kOutput, calls=%fused_computation.3 | convolution fusion | flops 268435456 | bytes 8404992 | tf_op jit(solution)/shard_map/mab,qmbc->qmac/dot_general | solution.py:21
  18.5 0.0 copy-start.2
  18.5 5.4 %fusion.5 = bf16[2,256,64,64]{1,3,2,0:T(8,128)(2,1)} fusion(bf16[2,256,64,64]{1,3,2,0:T(8,128)(2,1)S(1)} %fusion.3, bf16[2,64,64]{2,1,0:T(8,128)(2,1)S(1)} %copy-done.1), kind=kOutput, calls=%fused_computation.5 | convolution fusion | flops 270532608 | bytes 8404992 | tf_op jit(solution)/shard_map/qmac,mcd->qmad/dot_general | solution.py:24
  23.8 0.0 collective-permute-start.3
  23.8 4.1 %collective-permute-start = (bf16[256,8192]{0,1:T(8,128)(2,1)}, bf16[256,8192]{0,1:T(8,128)(2,1)}, u32[]{:S(2)}, u32[]{:S(2)}) collective-permute-start(bf16[256,8192]{0,1:T(8,128)(2,1)} %bitcast.6), channel_id=1, source_target_pairs={{0,248},{8,0},{16,8},{24,16},{32,24},{40,32},{48,40},{56,48},{64,5... | collective-permute-start | bytes 12582920 | tf_op jit(solution)/shard_map/ppermute | solution.py:13
  28.0 0.0 collective-permute-start.1
  28.0 0.5 collective-permute-start.4
  28.5 0.1 slice_convert_fusion.1
  28.6 0.1 broadcast_in_dim.7
  28.7 0.3 reshape.19
  29.0 45.6 %collective-permute-done.4 = s32[8,24]{1,0:T(8,128)S(1)} collective-permute-done((s32[8,24]{1,0:T(8,128)S(1)}, s32[8,24]{1,0:T(8,128)S(1)}, u32[]{:S(2)}, u32[]{:S(2)}) %collective-permute-start.4) | collective-permute-done | bytes 800 | tf_op jit(solution)/shard_map/ppermute | solution.py:13
  74.6 0.1 slice_convert_fusion
  74.6 0.1 broadcast_in_dim.8
  74.8 0.3 reshape.20
  75.1 0.0 collective-permute-done.1
  75.1 0.1 broadcast_in_dim.6
  75.2 0.3 reshape.18
  75.5 0.0 collective-permute-done.3
  75.5 0.0 slice-start
  75.5 7.2 %convolution_multiply_fusion = f32[256,512]{1,0:T(8,128)S(1)} fusion(f32[256,512]{1,0:T(8,128)S(1)} %reshape.20, bf16[256,8192]{0,1:T(8,128)(2,1)} %collective-permute-done.3, bf16[512,8192]{1,0:T(8,128)(2,1)} %param.8), kind=kOutput, calls=%fused_computation.7 | convolution fusion | flops 2147614720 | bytes 13631488 | tf_op jit(solution)/shard_map/dot_general | solution.py:37
  82.7 0.0 slice-start.1
  82.7 3.7 %collective-permute-start.5 = (f32[256,512]{1,0:T(8,128)S(1)}, f32[256,512]{1,0:T(8,128)S(1)}, u32[]{:S(2)}, u32[]{:S(2)}) collective-permute-start(f32[256,512]{1,0:T(8,128)S(1)} %convolution_multiply_fusion), channel_id=1, source_target_pairs={{0,248},{8,0},{16,8},{24,16},{32,24},{40,32},{48,40},{56,48},{64,5... | collective-permute-start | bytes 1572872 | tf_op jit(solution)/shard_map/ppermute | solution.py:13
  86.4 0.0 collective-permute-done
  86.4 7.0 %convolution_multiply_fusion.2 = f32[256,512]{1,0:T(8,128)S(1)} fusion(f32[256,512]{1,0:T(8,128)S(1)} %reshape.18, bf16[256,8192]{0,1:T(8,128)(2,1)} %collective-permute-done, bf16[512,8192]{1,0:T(8,128)(2,1)} %param.8), kind=kOutput, calls=%fused_computation.10 | convolution fusion | flops 2147614720 | bytes 13631488 | tf_op jit(solution)/shard_map/dot_general | solution.py:37
  93.5 45.5 %collective-permute-start.2 = (f32[256,512]{1,0:T(8,128)S(1)}, f32[256,512]{1,0:T(8,128)S(1)}, u32[]{:S(2)}, u32[]{:S(2)}) collective-permute-start(f32[256,512]{1,0:T(8,128)S(1)} %convolution_multiply_fusion.2), channel_id=1, source_target_pairs={{0,8},{8,16},{16,24},{24,32},{32,40},{40,48},{48,56},{56,64},{64,7... | collective-permute-start | bytes 1572872 | tf_op jit(solution)/shard_map/ppermute | solution.py:13
  139.0 4.6 %fusion.8 = f32[1,256,512]{2,1,0:T(8,128)S(1)} fusion(f32[256,512]{1,0:T(8,128)S(1)} %reshape.19, bf16[256,8192]{0,1:T(8,128)(2,1)} %bitcast.6, bf16[512,8192]{1,0:T(8,128)(2,1)S(1)} %bitcast.39), kind=kOutput, calls=%fused_computation.9 | convolution fusion | flops 2147614720 | bytes 13631488 | tf_op jit(solution)/shard_map/dot_general | solution.py:37
  143.6 0.0 collective-permute-done.5
  143.6 5.6 %collective-permute-done.2 = f32[256,512]{1,0:T(8,128)S(1)} collective-permute-done((f32[256,512]{1,0:T(8,128)S(1)}, f32[256,512]{1,0:T(8,128)S(1)}, u32[]{:S(2)}, u32[]{:S(2)}) %collective-permute-start.2) | collective-permute-done | bytes 524320 | tf_op jit(solution)/shard_map/ppermute | solution.py:13
  149.3 1.3 pad_maximum_fusion
  150.5 0.0 reduce-scatter.2.cloned.1.call-update
  150.6 46.9 %reduce-scatter.2.cloned.1.call-done = f32[3,32,512]{2,1,0:T(8,128)} async-done(((f32[3,256,512]{2,1,0:T(8,128)}), f32[3,32,512]{2,1,0:T(8,128)}) %reduce-scatter.2.cloned.1.call-update) | async-done | bytes 196624 | tf_op jit(solution)/shard_map/reduce_scatter | solution.py:53
  (10 shorter events, 0.0 us)
Async XLA Ops:
  6.5 6.4 %copy-start = (bf16[2,64,64]{2,1,0:T(8,128)(2,1)S(1)}, bf16[2,64,64]{2,1,0:T(8,128)(2,1)}, u32[]{:S(2)}) copy-start(bf16[2,64,64]{2,1,0:T(8,128)(2,1)} %param.6) | copy-start | bytes 49156
  6.5 190.9 %reduce-scatter.2.cloned.1.call-start = ((), (), s32[]{:S(2)}) async-start(), calls=%async_computation.1 | async-start | bytes 1769472 | tf_op jit(solution)/shard_map/reduce_scatter | solution.py:53
  12.9 5.5 %copy-start.1 = (bf16[2,64,64]{2,1,0:T(8,128)(2,1)S(1)}, bf16[2,64,64]{2,1,0:T(8,128)(2,1)}, u32[]{:S(2)}) copy-start(bf16[2,64,64]{2,1,0:T(8,128)(2,1)} %param.7) | copy-start | bytes 49156
  18.5 9.5 %copy-start.2 = (s32[8,24]{1,0:T(8,128)S(1)}, s32[8,24]{1,0:T(8,128)}, u32[]{:S(2)}) copy-start(s32[8,24]{1,0:T(8,128)} %param.9) | copy-start | bytes 2308
  23.8 51.7 %collective-permute-start.3 = (bf16[256,8192]{0,1:T(8,128)(2,1)}, bf16[256,8192]{0,1:T(8,128)(2,1)}, u32[]{:S(2)}, u32[]{:S(2)}) collective-permute-start(bf16[256,8192]{0,1:T(8,128)(2,1)} %bitcast.6), channel_id=1, source_target_pairs={{0,8},{8,16},{16,24},{24,32},{32,40},{40,48},{48,56},{56,64},{64,7... | collective-permute-start | bytes 12582920 | tf_op jit(solution)/shard_map/ppermute | solution.py:13
  23.8 62.6 %collective-permute-start = (bf16[256,8192]{0,1:T(8,128)(2,1)}, bf16[256,8192]{0,1:T(8,128)(2,1)}, u32[]{:S(2)}, u32[]{:S(2)}) collective-permute-start(bf16[256,8192]{0,1:T(8,128)(2,1)} %bitcast.6), channel_id=1, source_target_pairs={{0,248},{8,0},{16,8},{24,16},{32,24},{40,32},{48,40},{56,48},{64,5... | collective-permute-start | bytes 12582920 | tf_op jit(solution)/shard_map/ppermute | solution.py:13
  28.0 47.1 %collective-permute-start.1 = (s32[8,24]{1,0:T(8,128)S(1)}, s32[8,24]{1,0:T(8,128)S(1)}, u32[]{:S(2)}, u32[]{:S(2)}) collective-permute-start(s32[8,24]{1,0:T(8,128)S(1)} %copy-done.2), channel_id=1, source_target_pairs={{0,248},{8,0},{16,8},{24,16},{32,24},{40,32},{48,40},{56,48},{64,5... | collective-permute-start | bytes 2312 | tf_op jit(solution)/shard_map/ppermute | solution.py:13
  28.0 46.6 %collective-permute-start.4 = (s32[8,24]{1,0:T(8,128)S(1)}, s32[8,24]{1,0:T(8,128)S(1)}, u32[]{:S(2)}, u32[]{:S(2)}) collective-permute-start(s32[8,24]{1,0:T(8,128)S(1)} %copy-done.2), channel_id=1, source_target_pairs={{0,8},{8,16},{16,24},{24,32},{32,40},{40,48},{48,56},{56,64},{64,7... | collective-permute-start | bytes 2312 | tf_op jit(solution)/shard_map/ppermute | solution.py:13
  75.5 63.5 %slice-start = ((s8[8388608]{0:T(1024)(128)(4,1)}), s8[4194304]{0:T(1024)(128)(4,1)S(1)}, s32[]{:S(2)}) async-start(s8[8388608]{0:T(1024)(128)(4,1)} %bitcast.38), calls=%async_computation.2 | async-start | bytes 8388608
  82.7 56.3 %slice-start.1 = ((s8[8388608]{0:T(1024)(128)(4,1)}), s8[4194304]{0:T(1024)(128)(4,1)S(1)}, s32[]{:S(2)}) async-start(s8[8388608]{0:T(1024)(128)(4,1)} %bitcast.38), calls=%async_computation.3 | async-start | bytes 8388608
  82.7 60.9 %collective-permute-start.5 = (f32[256,512]{1,0:T(8,128)S(1)}, f32[256,512]{1,0:T(8,128)S(1)}, u32[]{:S(2)}, u32[]{:S(2)}) collective-permute-start(f32[256,512]{1,0:T(8,128)S(1)} %convolution_multiply_fusion), channel_id=1, source_target_pairs={{0,248},{8,0},{16,8},{24,16},{32,24},{40,32},{48,40},{56,48},{64,5... | collective-permute-start | bytes 1572872 | tf_op jit(solution)/shard_map/ppermute | solution.py:13
  93.5 55.8 %collective-permute-start.2 = (f32[256,512]{1,0:T(8,128)S(1)}, f32[256,512]{1,0:T(8,128)S(1)}, u32[]{:S(2)}, u32[]{:S(2)}) collective-permute-start(f32[256,512]{1,0:T(8,128)S(1)} %convolution_multiply_fusion.2), channel_id=1, source_target_pairs={{0,8},{8,16},{16,24},{24,32},{32,40},{40,48},{48,56},{56,64},{64,7... | collective-permute-start | bytes 1572872 | tf_op jit(solution)/shard_map/ppermute | solution.py:13
Sparse Core Ops, SparseCore 0:
  150.7 46.7 reduce-scatter.1
where the time goes:
time: 205 us; the launch traced here: 204 us
  waiting for transfers between devices  98.2 us (48%)
  starting transfers between devices  53.9 us (26%)
  matrix products  29.6 us (14%)
  between operations  13.5 us (7%)
  local copies, waits for them, and re-layouts  7.62 us (4%)
    ppermute x6, starting transfers between devices, shifted(): return lax.ppermute(value, axis, pairs)  53.9 us
    ppermute x6, waiting for transfers between devices, shifted(): return lax.ppermute(value, axis, pairs)  51.2 us
    reduce_scatter x1, waiting for transfers between devices, body(): summed = lax.psum_scatter(stacked, 'grp', scatter_dimension=1, tiled=True)  46.9 us
    dot_general x3, matrix products, score(): lax.dot_general(ready, slab, (((1,), (1,)), ((), ())), preferred_element_...  18.8 us
    unnamed x11, local copies, waits for them, and re-layouts  6.41 us
    dot_general x1, matrix products, precondition(): jnp.einsum('mab,qmbc->qmac', inv_in, query_part, preferred_element_type=j...  5.51 us
    dot_general x1, matrix products, precondition(): jnp.einsum('qmac,mcd->qmad', left, inv_out, preferred_element_type=jnp.fl...  5.35 us
  transfers between devices with their start and end apart: 7, of which 3 were waited for; matrix products, arithmetic and copies ran while one was open for 10% of the time, Pallas kernels for 0%

commit v1 on v0

v1 whole, which is shorter than its diff:
```python
import functools

import jax
import jax.numpy as jnp
from jax import lax
from jax.experimental import pallas as pl
from jax.experimental.pallas import tpu as pltpu
from jax.sharding import PartitionSpec as P

MESH = pl.DeviceIdType.MESH
F32 = jnp.float32
BF16 = jnp.bfloat16
QB = 32
SUB = 64
SELF, PARTNER, CROSS = 0, 1, 2
GROUP = 8


def nt_dot(a, b):
    return lax.dot_general(a, b, (((1,), (1,)), ((), ())), preferred_element_type=F32)


def iota(shape, dim):
    return lax.broadcasted_iota(jnp.int32, shape, dim)


def one_hot(cond):
    return jnp.where(cond, 1.0, 0.0).astype(BF16)


def place(a, b):
    return jnp.dot(a, b, preferred_element_type=F32).astype(BF16)


def split_factor(matrix, side):
    half = side // 2
    row = iota((side, side), 0)
    col = iota((side, side), 1)
    rows = one_hot(col == 2 * (row % half) + row // half)
    straight = one_hot(row == 2 * (col % half) + col // half)
    swapped = one_hot(row == 2 * (col % half) + 1 - col // half)
    picked = place(rows, matrix)
    upper = place(picked, straight)
    lower = place(picked, swapped)
    return jnp.where(row < half, upper.astype(F32), lower.astype(F32)).astype(BF16)


def twice(matrix, side):
    wide = 2 * side
    rows = one_hot(iota((wide, side), 0) % side == iota((wide, side), 1))
    cols = one_hot(iota((side, wide), 0) == iota((side, wide), 1) % side)
    full = place(place(rows, matrix), cols)
    same = iota((wide, wide), 0) // side == iota((wide, wide), 1) // side
    return jnp.where(same, full.astype(F32), 0.0).astype(BF16)


def kernel(
    n_ex, n_x,
    q_hbm, in_ref, out_ref, s_hbm, listed_ref, o_ref,
    raw, vraw, vis, slab, part, hop, mine, last, left_w, right_w, spread, gather, mask,
    raw_sem, slab_sem, vraw_send, vraw_recv, send_sem, recv_sem, hop_send, hop_recv, last_send, last_recv,
):
    modules, side, _ = in_ref.shape
    pairs = side // 2
    wide = 2 * side
    n_chunk = raw.shape[0]
    b = lax.axis_index("ex")
    g = lax.axis_index("grp")
    yl = g // n_x
    x = lax.rem(g, n_x)
    par = lax.rem(b, 2)
    partner = b + 1 - 2 * par
    cross = lax.rem(b - 1 + 2 * par + n_ex, n_ex)
    other = (1 - yl) * n_x + x

    def order(t):
        d = 1 + t // 2
        rel = lax.rem(t, 2)
        to_x = lax.rem(x + d, n_x)
        to_y = lax.rem(yl + rel, 2)
        return d, rel, to_x, to_y * n_x + to_x

    peers = [(b, other), (partner, g), (partner, other), (cross, g), (cross, other)]
    peers += [(b, yl * n_x + lax.rem(x + d, n_x)) for d in range(1, n_x)]
    barrier = pltpu.get_barrier_semaphore()
    for peer in peers:
        pl.semaphore_signal(barrier, inc=1, device_id=peer, device_id_type=MESH)

    def load_raw(t):
        j = order(t)[3]
        return pltpu.make_async_copy(q_hbm.at[pl.ds(pl.multiple_of(j * QB, QB), QB)], raw.at[j], raw_sem.at[t])

    for t in range(n_chunk):
        load_raw(t).start()
    slab_copy = pltpu.make_async_copy(s_hbm, slab, slab_sem)
    slab_copy.start()

    pl.semaphore_wait(barrier, len(peers))

    first = order(0)[3]
    raw_out = pltpu.make_async_remote_copy(
        q_hbm.at[pl.ds(pl.multiple_of(first * QB, QB), QB)], vraw, vraw_send, vraw_recv,
        device_id=(cross, g), device_id_type=MESH)
    raw_out.start()

    for m in range(modules):
        left_w[m] = split_factor(in_ref[m], side)
        right_w[m] = twice(out_ref[m], side)
    rows_l = listed_ref.shape[0]
    row = jnp.sum(
        jnp.where(iota(listed_ref.shape, 0) == g, listed_ref[...].astype(F32), 0.0), axis=0, keepdims=True)
    widths = (listed_ref.shape[1], mask.shape[1])
    fan = one_hot(iota(widths, 1) // SUB == iota(widths, 0))
    mask[...] = jnp.dot(
        jnp.broadcast_to(row, listed_ref.shape).astype(BF16), fan, preferred_element_type=F32)

    low = (iota((pairs, GROUP * wide), 1) % wide) < side

    def precondition(src, dst):
        for m in range(modules):
            base = m * side * side
            for p in range(pairs):
                spread[pl.ds(p, QB, stride=pairs), :] = src[:, base + p * wide:base + (p + 1) * wide].astype(F32)
            for q in range(0, QB, GROUP):
                rows = spread[q * pairs:(q + GROUP) * pairs, :]
                turned = pltpu.roll(rows, side, 1).astype(BF16)
                rows = rows.astype(BF16)
                lay = lambda v: jnp.concatenate([v[i * pairs:(i + 1) * pairs] for i in range(GROUP)], axis=1)
                both = jnp.concatenate([lay(rows), lay(turned)], axis=0)
                left = jnp.dot(left_w[m], both, preferred_element_type=F32)
                left = jnp.where(low, left[:pairs], left[pairs:]).astype(BF16)
                stack = jnp.concatenate([left[:, i * wide:(i + 1) * wide] for i in range(GROUP)], axis=0)
                gather[q * pairs:(q + GROUP) * pairs, :] = jnp.dot(stack, right_w[m], preferred_element_type=F32)
            for p in range(pairs):
                dst[:, base + p * wide:base + (p + 1) * wide] = gather[pl.ds(p, QB, stride=pairs), :].astype(BF16)

    def to_partner(j):
        return pltpu.make_async_remote_copy(
            vis.at[SELF, j], vis.at[PARTNER, j], send_sem.at[0, j], recv_sem.at[0, j],
            device_id=(partner, g), device_id_type=MESH)

    def to_cross(j):
        return pltpu.make_async_remote_copy(
            vis.at[SELF, j], vis.at[CROSS, j], send_sem.at[1, j], recv_sem.at[1, j],
            device_id=(cross, g), device_id_type=MESH)

    def prepare(t, carry):
        j = order(t)[3]
        load_raw(t).wait()
        precondition(raw.at[j], vis.at[SELF, j])

        @pl.when(t > 0)
        def _():
            to_cross(j).start()

        to_partner(j).start()
        return carry

    lax.fori_loop(0, n_chunk, prepare, 0)
    slab_copy.wait()

    depth = slab.shape[1]
    step = 1024

    def to_hop(w, t):
        d, rel, to_x, j = order(t)
        return pltpu.make_async_remote_copy(
            part.at[w, t], hop.at[w, rel, n_x - 1 - d], hop_send.at[w, t], hop_recv.at[w, rel, n_x - 1 - d],
            device_id=(b, yl * n_x + to_x), device_id_type=MESH)

    def score(w, t):
        j = order(t)[3]

        def inner(k, acc):
            at = pl.ds(pl.multiple_of(k * step, step), step)
            return acc + nt_dot(vis[w, j, :, at], slab[:, at])

        part[w, t] = lax.fori_loop(0, depth // step, inner, jnp.zeros(part.shape[2:], F32))

        @pl.when(t < n_chunk - 2)
        def _():
            to_hop(w, t).start()

    def own(t, carry):
        score(SELF, t)
        return carry

    def near(t, carry):
        to_partner(order(t)[3]).wait_recv()
        score(PARTNER, t)
        return carry

    def far(t, carry):
        to_cross(order(t)[3]).wait_recv()
        score(CROSS, t)
        return carry

    owner = (b, partner, cross)

    def to_last(w, rel):
        return pltpu.make_async_remote_copy(
            mine.at[w, rel], last.at[w, rel], last_send.at[w, rel], last_recv.at[w, rel],
            device_id=(owner[w], g if rel == 0 else other), device_id_type=MESH)

    def gather_x(w, rel):
        for d in range(1, n_x):
            to_hop(w, 2 * (d - 1) + rel).wait_recv()
        total = part[w, n_chunk - 2 + rel]
        for d in range(n_x - 1):
            total = total + hop[w, rel, d]
        mine[w, rel] = total
        if not (w == SELF and rel == 0):
            to_last(w, rel).start()

    def finish(w):
        width = part.shape[3]
        to_last(w, 1).wait_recv()
        if w == SELF:
            total = mine[w, 0] + last[w, 1]
            o_ref[1] = total * mask[0:1, width:2 * width]
            return
        to_last(w, 0).wait_recv()
        total = last[w, 0] + last[w, 1]
        upper = par == (1 if w == CROSS else 0)

        @pl.when(upper)
        def _():
            o_ref[2] = total * mask[0:1, 2 * width:3 * width]

        @pl.when(jnp.logical_not(upper))
        def _():
            o_ref[0] = total * mask[0:1, 0:width]

    lax.fori_loop(0, n_chunk, own, 0)
    lax.fori_loop(0, n_chunk, near, 0)

    raw_out.wait_recv()
    precondition(vraw, vis.at[CROSS, first])
    score(CROSS, 0)
    lax.fori_loop(1, 3, far, 0)
    for w in (SELF, PARTNER):
        for rel in range(2):
            gather_x(w, rel)
    lax.fori_loop(3, 5, far, 0)
    finish(SELF)
    finish(PARTNER)
    lax.fori_loop(5, n_chunk - 1, far, 0)
    gather_x(CROSS, 0)
    far(n_chunk - 1, 0)
    gather_x(CROSS, 1)

    raw_out.wait_send()

    def drain(t, carry):
        j = order(t)[3]
        to_partner(j).wait_send()

        @pl.when(t > 0)
        def _():
            to_cross(j).wait_send()

        @pl.when(t < n_chunk - 2)
        def _():
            for w in range(3):
                to_hop(w, t).wait_send()

        return carry

    lax.fori_loop(0, n_chunk, drain, 0)
    finish(CROSS)
    for w in range(3):
        for rel in range(2):
            if not (w == SELF and rel == 0):
                to_last(w, rel).wait_send()


def solution(mesh):
    n_ex = mesh.shape["ex"]
    n_grp = mesh.shape["grp"]
    n_x = n_grp // 2

    def body(queries, inv_in, inv_out, store, listed):
        count, dims = queries.shape
        examples = store.shape[0]
        n_chunk = count // QB
        modules, side, _ = inv_in.shape
        tile = (QB, examples)
        vmem = pl.BlockSpec(memory_space=pltpu.VMEM)
        hbm = pl.BlockSpec(memory_space=pl.ANY)
        dma = pltpu.SemaphoreType.DMA
        return pl.pallas_call(
            functools.partial(kernel, n_ex, n_x),
            out_shape=jax.ShapeDtypeStruct((3,) + tile, F32),
            in_specs=[hbm, vmem, vmem, hbm, vmem],
            out_specs=vmem,
            scratch_shapes=[
                pltpu.VMEM((n_chunk, QB, dims), BF16),
                pltpu.VMEM((QB, dims), BF16),
                pltpu.VMEM((3, n_chunk, QB, dims), BF16),
                pltpu.VMEM((examples, dims), BF16),
                pltpu.VMEM((3, n_chunk) + tile, F32),
                pltpu.VMEM((3, 2, n_x - 1) + tile, F32),
                pltpu.VMEM((3, 2) + tile, F32),
                pltpu.VMEM((3, 2) + tile, F32),
                pltpu.VMEM((modules, side, side), BF16),
                pltpu.VMEM((modules, 2 * side, 2 * side), BF16),
                pltpu.VMEM((QB * side // 2, 2 * side), F32),
                pltpu.VMEM((QB * side // 2, 2 * side), F32),
                pltpu.VMEM((listed.shape[0], listed.shape[1] * SUB), F32),
                dma((n_chunk,)),
                dma,
                dma,
                dma,
                dma((2, n_chunk)),
                dma((2, n_chunk)),
                dma((3, n_chunk)),
                dma((3, 2, n_x - 1)),
                dma((3, 2)),
                dma((3, 2)),
            ],
            compiler_params=pltpu.CompilerParams(
                collective_id=0, has_side_effects=True, vmem_limit_bytes=60 * 2**20),
        )(queries, inv_in, inv_out, store, listed)

    in_specs = (
        P("ex", "grp"),
        P("grp", None, None),
        P("grp", None, None),
        P("ex", "grp"),
        P("ex", None),
    )
    out_specs = P(None, ("ex", "grp"), None)
    return jax.shard_map(body, mesh=mesh, in_specs=in_specs, out_specs=out_specs, check_vma=False)
```

time: 205 us -> 121 us (0.59)
  the two profiles are of different devices: /device:TPU:32 before, /device:TPU:2 now
where the time goes in v1:
time: 121 us
  Pallas kernels  119 us (98%)
  local copies, waits for them, and re-layouts  1.62 us (1%)
    pallas_call x1, Pallas kernels, body(): pl.pallas_call(functools.partial(kernel, n_ex, n_x), out_shape=jax.ShapeD...  119 us

profile of v1, /device:TPU:2, one launch (start us, length us, event | category | flops | bytes accessed | tf_op | source)
XLA Modules:
  0.0 120.7 jit_solution(6908187234880296625)
XLA Ops:
  0.0 119.1 %shard_map.55 = f32[3,32,512]{2,1,0:T(8,128)} custom-call(bf16[256,8192]{1,0:T(8,128)(2,1)} %q_hbm.1, bf16[2,64,64]{2,1,0:T(8,128)(2,1)} %in_ref.1, bf16[2,64,64]{2,1,0:T(8,128)(2,1)} %out_ref.1, bf16[512,8192]{1,0:T(8,128)(2,1)} %s_hbm.1, s32[8,24]{1,0:T(8,128)} %listed_ref.1), custom_call_target="tpu_custom_call" | custom-call | tf_op jit(solution)/shard_map/pallas_call | solution.py:291
  119.1 1.6 %copy.7 = f32[3,32,512]{2,1,0:T(8,128)} copy(f32[3,32,512]{2,1,0:T(8,128)} %shard_map.55) | data formatting | bytes 393216

commit v2 on v1

--- a/solution.py
+++ b/solution.py
@@ -14,6 +14,7 @@
 SUB = 64
 SELF, PARTNER, CROSS = 0, 1, 2
 GROUP = 8
+PIECES = 4
 
 
 def nt_dot(a, b):
@@ -58,12 +59,13 @@
     n_ex, n_x,
     q_hbm, in_ref, out_ref, s_hbm, listed_ref, o_ref,
     raw, vraw, vis, slab, part, hop, mine, last, left_w, right_w, spread, gather, mask,
-    raw_sem, slab_sem, vraw_send, vraw_recv, send_sem, recv_sem, hop_send, hop_recv, last_send, last_recv,
+    raw_sem, slab_sem, vraw_send, vraw_recv, near_send, near_recv, far_send, far_recv, hop_send, hop_recv, last_send, last_recv,
 ):
     modules, side, _ = in_ref.shape
     pairs = side // 2
     wide = 2 * side
-    n_chunk = raw.shape[0]
+    n_chunk = raw.shape[0] // QB
+    depth = slab.shape[1]
     b = lax.axis_index("ex")
     g = lax.axis_index("grp")
     yl = g // n_x
@@ -86,9 +88,11 @@
     for peer in peers:
         pl.semaphore_signal(barrier, inc=1, device_id=peer, device_id_type=MESH)
 
+    def rows_of(t):
+        return pl.ds(pl.multiple_of(order(t)[3] * QB, QB), QB)
+
     def load_raw(t):
-        j = order(t)[3]
-        return pltpu.make_async_copy(q_hbm.at[pl.ds(pl.multiple_of(j * QB, QB), QB)], raw.at[j], raw_sem.at[t])
+        return pltpu.make_async_copy(q_hbm.at[rows_of(t)], raw.at[rows_of(t)], raw_sem.at[t])
 
     for t in range(n_chunk):
         load_raw(t).start()
@@ -97,9 +101,8 @@
 
     pl.semaphore_wait(barrier, len(peers))
 
-    first = order(0)[3]
     raw_out = pltpu.make_async_remote_copy(
-        q_hbm.at[pl.ds(pl.multiple_of(first * QB, QB), QB)], vraw, vraw_send, vraw_recv,
+        q_hbm.at[rows_of(0)], vraw, vraw_send, vraw_recv,
         device_id=(cross, g), device_id_type=MESH)
     raw_out.start()
 
@@ -134,65 +137,73 @@
             for p in range(pairs):
                 dst[:, base + p * wide:base + (p + 1) * wide] = gather[pl.ds(p, QB, stride=pairs), :].astype(BF16)
 
-    def to_partner(j):
+    piece = depth // PIECES
+
+    def to_partner(t):
         return pltpu.make_async_remote_copy(
-            vis.at[SELF, j], vis.at[PARTNER, j], send_sem.at[0, j], recv_sem.at[0, j],
+            vis.at[SELF, rows_of(t)], vis.at[PARTNER, rows_of(t)], near_send.at[t], near_recv.at[t],
             device_id=(partner, g), device_id_type=MESH)
 
-    def to_cross(j):
+    def columns(k):
+        return pl.ds(pl.multiple_of(k * piece, piece), piece)
+
+    def to_cross(t, k):
         return pltpu.make_async_remote_copy(
-            vis.at[SELF, j], vis.at[CROSS, j], send_sem.at[1, j], recv_sem.at[1, j],
-            device_id=(cross, g), device_id_type=MESH)
+            vis.at[SELF, rows_of(t), columns(k)], vis.at[CROSS, rows_of(t), columns(k)],
+            far_send.at[t, k], far_recv.at[t, k], device_id=(cross, g), device_id_type=MESH)
 
     def prepare(t, carry):
-        j = order(t)[3]
         load_raw(t).wait()
-        precondition(raw.at[j], vis.at[SELF, j])
+        precondition(raw.at[rows_of(t)], vis.at[SELF, rows_of(t)])
 
         @pl.when(t > 0)
         def _():
-            to_cross(j).start()
-
-        to_partner(j).start()
+            for k in range(PIECES):
+                to_cross(t, k).start()
+
+        to_partner(t).start()
         return carry
 
     lax.fori_loop(0, n_chunk, prepare, 0)
     slab_copy.wait()
-
-    depth = slab.shape[1]
-    step = 1024
 
     def to_hop(w, t):
         d, rel, to_x, j = order(t)
         return pltpu.make_async_remote_copy(
-            part.at[w, t], hop.at[w, rel, n_x - 1 - d], hop_send.at[w, t], hop_recv.at[w, rel, n_x - 1 - d],
+            part.at[w, rows_of(t)], hop.at[w, rel, n_x - 1 - d], hop_send.at[w, t], hop_recv.at[w, rel, n_x - 1 - d],
             device_id=(b, yl * n_x + to_x), device_id_type=MESH)
 
-    def score(w, t):
-        j = order(t)[3]
+    def score_all(w):
+        part[w] = nt_dot(vis[w, :, 0:piece], slab[:, 0:piece])
+
+        def inner(k, carry):
+            part[w] += nt_dot(vis[w, :, columns(k)], slab[:, columns(k)])
+            return carry
+
+        lax.fori_loop(1, PIECES, inner, 0)
+
+        def send(t, carry):
+            to_hop(w, t).start()
+            return carry
+
+        lax.fori_loop(0, n_chunk - 2, send, 0)
+
+    def far(t, arrives):
+        rows = rows_of(t)
 
         def inner(k, acc):
-            at = pl.ds(pl.multiple_of(k * step, step), step)
-            return acc + nt_dot(vis[w, j, :, at], slab[:, at])
-
-        part[w, t] = lax.fori_loop(0, depth // step, inner, jnp.zeros(part.shape[2:], F32))
+            if arrives:
+                to_cross(t, k).wait_recv()
+            return acc + nt_dot(vis[CROSS, rows, columns(k)], slab[:, columns(k)])
+
+        part[CROSS, rows] = lax.fori_loop(0, PIECES, inner, jnp.zeros((QB, part.shape[2]), F32))
 
         @pl.when(t < n_chunk - 2)
         def _():
-            to_hop(w, t).start()
-
-    def own(t, carry):
-        score(SELF, t)
-        return carry
-
-    def near(t, carry):
-        to_partner(order(t)[3]).wait_recv()
-        score(PARTNER, t)
-        return carry
-
-    def far(t, carry):
-        to_cross(order(t)[3]).wait_recv()
-        score(CROSS, t)
+            to_hop(CROSS, t).start()
+
+    def far_step(t, carry):
+        far(t, True)
         return carry
 
     owner = (b, partner, cross)
@@ -205,7 +216,7 @@
     def gather_x(w, rel):
         for d in range(1, n_x):
             to_hop(w, 2 * (d - 1) + rel).wait_recv()
-        total = part[w, n_chunk - 2 + rel]
+        total = part[w, rows_of(n_chunk - 2 + rel)]
         for d in range(n_x - 1):
             total = total + hop[w, rel, d]
         mine[w, rel] = total
@@ -213,7 +224,7 @@
             to_last(w, rel).start()
 
     def finish(w):
-        width = part.shape[3]
+        width = part.shape[2]
         to_last(w, 1).wait_recv()
         if w == SELF:
             total = mine[w, 0] + last[w, 1]
@@ -231,33 +242,34 @@
         def _():
             o_ref[0] = total * mask[0:1, 0:width]
 
-    lax.fori_loop(0, n_chunk, own, 0)
-    lax.fori_loop(0, n_chunk, near, 0)
-
-    raw_out.wait_recv()
-    precondition(vraw, vis.at[CROSS, first])
-    score(CROSS, 0)
-    lax.fori_loop(1, 3, far, 0)
+    score_all(SELF)
+    for t in range(n_chunk):
+        to_partner(t).wait_recv()
+    score_all(PARTNER)
+
     for w in (SELF, PARTNER):
         for rel in range(2):
             gather_x(w, rel)
-    lax.fori_loop(3, 5, far, 0)
+
+    raw_out.wait_recv()
+    precondition(vraw, vis.at[CROSS, rows_of(0)])
+    far(0, False)
+    lax.fori_loop(1, n_chunk - 1, far_step, 0)
+    gather_x(CROSS, 0)
+    far(n_chunk - 1, True)
+    gather_x(CROSS, 1)
     finish(SELF)
     finish(PARTNER)
-    lax.fori_loop(5, n_chunk - 1, far, 0)
-    gather_x(CROSS, 0)
-    far(n_chunk - 1, 0)
-    gather_x(CROSS, 1)
 
     raw_out.wait_send()
 
     def drain(t, carry):
-        j = order(t)[3]
-        to_partner(j).wait_send()
+        to_partner(t).wait_send()
 
         @pl.when(t > 0)
         def _():
-            to_cross(j).wait_send()
+            for k in range(PIECES):
+                to_cross(t, k).wait_send()
 
         @pl.when(t < n_chunk - 2)
         def _():
@@ -294,11 +306,11 @@
             in_specs=[hbm, vmem, vmem, hbm, vmem],
             out_specs=vmem,
             scratch_shapes=[
-                pltpu.VMEM((n_chunk, QB, dims), BF16),
+                pltpu.VMEM((count, dims), BF16),
                 pltpu.VMEM((QB, dims), BF16),
-                pltpu.VMEM((3, n_chunk, QB, dims), BF16),
+                pltpu.VMEM((3, count, dims), BF16),
                 pltpu.VMEM((examples, dims), BF16),
-                pltpu.VMEM((3, n_chunk) + tile, F32),
+                pltpu.VMEM((3, count, examples), F32),
                 pltpu.VMEM((3, 2, n_x - 1) + tile, F32),
                 pltpu.VMEM((3, 2) + tile, F32),
                 pltpu.VMEM((3, 2) + tile, F32),
@@ -311,8 +323,10 @@
                 dma,
                 dma,
                 dma,
-                dma((2, n_chunk)),
-                dma((2, n_chunk)),
+                dma((n_chunk,)),
+                dma((n_chunk,)),
+                dma((n_chunk, PIECES)),
+                dma((n_chunk, PIECES)),
                 dma((3, n_chunk)),
                 dma((3, 2, n_x - 1)),
                 dma((3, 2)),

time: 121 us -> 109 us (0.901)
  the two profiles are of different devices: /device:TPU:2 before, /device:TPU:1 now
where the time goes in v2:
time: 109 us
  Pallas kernels  107 us (98%)
  local copies, waits for them, and re-layouts  1.62 us (1%)
    pallas_call x1, Pallas kernels, body(): pl.pallas_call(functools.partial(kernel, n_ex, n_x), out_shape=jax.ShapeD...  107 us

profile of v2, /device:TPU:1, one launch (start us, length us, event | category | flops | bytes accessed | tf_op | source)
XLA Modules:
  0.0 108.8 jit_solution(848765498891794960)
XLA Ops:
  0.0 107.1 %shard_map.55 = f32[3,32,512]{2,1,0:T(8,128)} custom-call(bf16[256,8192]{1,0:T(8,128)(2,1)} %q_hbm.1, bf16[2,64,64]{2,1,0:T(8,128)(2,1)} %in_ref.1, bf16[2,64,64]{2,1,0:T(8,128)(2,1)} %out_ref.1, bf16[512,8192]{1,0:T(8,128)(2,1)} %s_hbm.1, s32[8,24]{1,0:T(8,128)} %listed_ref.1), custom_call_target="tpu_custom_call" | custom-call | tf_op jit(solution)/shard_map/pallas_call | solution.py:303
  107.2 1.6 %copy.7 = f32[3,32,512]{2,1,0:T(8,128)} copy(f32[3,32,512]{2,1,0:T(8,128)} %shard_map.55) | data formatting | bytes 393216

commit v3 on v2

--- a/solution.py
+++ b/solution.py
@@ -14,7 +14,7 @@
 SUB = 64
 SELF, PARTNER, CROSS = 0, 1, 2
 GROUP = 8
-PIECES = 4
+PIECES = 8
 
 
 def nt_dot(a, b):
@@ -57,9 +57,9 @@
 
 def kernel(
     n_ex, n_x,
-    q_hbm, in_ref, out_ref, s_hbm, listed_ref, o_ref,
-    raw, vraw, vis, slab, part, hop, mine, last, left_w, right_w, spread, gather, mask,
-    raw_sem, slab_sem, vraw_send, vraw_recv, near_send, near_recv, far_send, far_recv, hop_send, hop_recv, last_send, last_recv,
+    q_hbm, in_hbm, out_hbm, s_hbm, listed_hbm, o_ref,
+    in_ref, out_ref, listed_ref, raw, vraw, vis, slab, part, hop, mine, last, left_w, right_w, spread, gather, mask,
+    small_sem, raw_sem, slab_sem, vraw_send, vraw_recv, near_send, near_recv, far_send, far_recv, hop_send, hop_recv, last_send, last_recv,
 ):
     modules, side, _ = in_ref.shape
     pairs = side // 2
@@ -94,6 +94,12 @@
     def load_raw(t):
         return pltpu.make_async_copy(q_hbm.at[rows_of(t)], raw.at[rows_of(t)], raw_sem.at[t])
 
+    small = [
+        pltpu.make_async_copy(source, target, small_sem.at[i])
+        for i, (source, target) in enumerate([(in_hbm, in_ref), (out_hbm, out_ref), (listed_hbm, listed_ref)])
+    ]
+    for copy in small:
+        copy.start()
     for t in range(n_chunk):
         load_raw(t).start()
     slab_copy = pltpu.make_async_copy(s_hbm, slab, slab_sem)
@@ -106,10 +112,11 @@
         device_id=(cross, g), device_id_type=MESH)
     raw_out.start()
 
+    for copy in small:
+        copy.wait()
     for m in range(modules):
         left_w[m] = split_factor(in_ref[m], side)
         right_w[m] = twice(out_ref[m], side)
-    rows_l = listed_ref.shape[0]
     row = jnp.sum(
         jnp.where(iota(listed_ref.shape, 0) == g, listed_ref[...].astype(F32), 0.0), axis=0, keepdims=True)
     widths = (listed_ref.shape[1], mask.shape[1])
@@ -219,7 +226,7 @@
         total = part[w, rows_of(n_chunk - 2 + rel)]
         for d in range(n_x - 1):
             total = total + hop[w, rel, d]
-        mine[w, rel] = total
+        mine[w, rel] = total.astype(mine.dtype)
         if not (w == SELF and rel == 0):
             to_last(w, rel).start()
 
@@ -227,11 +234,11 @@
         width = part.shape[2]
         to_last(w, 1).wait_recv()
         if w == SELF:
-            total = mine[w, 0] + last[w, 1]
+            total = mine[w, 0].astype(F32) + last[w, 1].astype(F32)
             o_ref[1] = total * mask[0:1, width:2 * width]
             return
         to_last(w, 0).wait_recv()
-        total = last[w, 0] + last[w, 1]
+        total = last[w, 0].astype(F32) + last[w, 1].astype(F32)
         upper = par == (1 if w == CROSS else 0)
 
         @pl.when(upper)
@@ -298,27 +305,31 @@
         modules, side, _ = inv_in.shape
         tile = (QB, examples)
         vmem = pl.BlockSpec(memory_space=pltpu.VMEM)
-        hbm = pl.BlockSpec(memory_space=pl.ANY)
+        hbm = pl.BlockSpec(memory_space=pltpu.HBM)
         dma = pltpu.SemaphoreType.DMA
         return pl.pallas_call(
             functools.partial(kernel, n_ex, n_x),
             out_shape=jax.ShapeDtypeStruct((3,) + tile, F32),
-            in_specs=[hbm, vmem, vmem, hbm, vmem],
+            in_specs=[hbm] * 5,
             out_specs=vmem,
             scratch_shapes=[
+                pltpu.VMEM(inv_in.shape, BF16),
+                pltpu.VMEM(inv_out.shape, BF16),
+                pltpu.VMEM(listed.shape, listed.dtype),
                 pltpu.VMEM((count, dims), BF16),
                 pltpu.VMEM((QB, dims), BF16),
                 pltpu.VMEM((3, count, dims), BF16),
                 pltpu.VMEM((examples, dims), BF16),
                 pltpu.VMEM((3, count, examples), F32),
                 pltpu.VMEM((3, 2, n_x - 1) + tile, F32),
-                pltpu.VMEM((3, 2) + tile, F32),
-                pltpu.VMEM((3, 2) + tile, F32),
+                pltpu.VMEM((3, 2) + tile, BF16),
+                pltpu.VMEM((3, 2) + tile, BF16),
                 pltpu.VMEM((modules, side, side), BF16),
                 pltpu.VMEM((modules, 2 * side, 2 * side), BF16),
                 pltpu.VMEM((QB * side // 2, 2 * side), F32),
                 pltpu.VMEM((QB * side // 2, 2 * side), F32),
                 pltpu.VMEM((listed.shape[0], listed.shape[1] * SUB), F32),
+                dma((3,)),
                 dma((n_chunk,)),
                 dma,
                 dma,
@@ -333,8 +344,8 @@
                 dma((3, 2)),
             ],
             compiler_params=pltpu.CompilerParams(
-                collective_id=0, has_side_effects=True, vmem_limit_bytes=60 * 2**20),
-        )(queries, inv_in, inv_out, store, listed)
+                collective_id=0, has_side_effects=True, vmem_limit_bytes=36 * 2**20),
+        )(*[pltpu.with_memory_space_constraint(v, pltpu.HBM) for v in (queries, inv_in, inv_out, store, listed)])
 
     in_specs = (
         P("ex", "grp"),

time: 109 us -> 105 us (0.963)
  Pallas kernels: 107 us -> 104 us
    pallas_call x1, Pallas kernels: 107 us -> 104 us  [body(): pl.pallas_call(functools.partial(kernel, n_ex, n_x), out_shape=jax.ShapeD...]
where the time goes in v3:
time: 105 us
  Pallas kernels  104 us (99%)
    pallas_call x1, Pallas kernels, body(): pl.pallas_call(functools.partial(kernel, n_ex, n_x), out_shape=jax.ShapeD...  104 us

profile of v3, /device:TPU:1, one launch (start us, length us, event | category | flops | bytes accessed | tf_op | source)
XLA Modules:
  0.0 104.9 jit_solution(8191672316088905881)
XLA Ops:
  0.0 104.2 %shard_map.55 = f32[3,32,512]{2,1,0:T(8,128)S(1)} custom-call(bf16[256,8192]{1,0:T(8,128)(2,1)} %q_hbm.1, bf16[2,64,64]{2,1,0:T(8,128)(2,1)} %in_hbm.1, bf16[2,64,64]{2,1,0:T(8,128)(2,1)} %out_hbm.1, bf16[512,8192]{1,0:T(8,128)(2,1)} %s_hbm.1, s32[8,24]{1,0:T(8,128)} %listed_hbm.1), custom_call_target="tpu_custom_call" | custom-call | tf_op jit(solution)/shard_map/pallas_call | solution.py:310
  104.2 0.7 copy.7

commit v4 on v3

--- a/solution.py
+++ b/solution.py
@@ -14,7 +14,8 @@
 SUB = 64
 SELF, PARTNER, CROSS = 0, 1, 2
 GROUP = 8
-PIECES = 8
+PIECES = (2, 4, 8, 16, 16)
+SPAN = 4096
 
 
 def nt_dot(a, b):
@@ -59,7 +60,7 @@
     n_ex, n_x,
     q_hbm, in_hbm, out_hbm, s_hbm, listed_hbm, o_ref,
     in_ref, out_ref, listed_ref, raw, vraw, vis, slab, part, hop, mine, last, left_w, right_w, spread, gather, mask,
-    small_sem, raw_sem, slab_sem, vraw_send, vraw_recv, near_send, near_recv, far_send, far_recv, hop_send, hop_recv, last_send, last_recv,
+    small_sem, raw_sem, slab_sem, vraw_send, vraw_recv, near_send, near_recv, far_send, far_recv, tail_recv, hop_send, hop_recv, last_send, last_recv,
 ):
     modules, side, _ = in_ref.shape
     pairs = side // 2
@@ -100,8 +101,8 @@
     ]
     for copy in small:
         copy.start()
-    for t in range(n_chunk):
-        load_raw(t).start()
+    for i in range(n_chunk):
+        load_raw((i + 1) % n_chunk).start()
     slab_copy = pltpu.make_async_copy(s_hbm, slab, slab_sem)
     slab_copy.start()
 
@@ -119,8 +120,8 @@
         right_w[m] = twice(out_ref[m], side)
     row = jnp.sum(
         jnp.where(iota(listed_ref.shape, 0) == g, listed_ref[...].astype(F32), 0.0), axis=0, keepdims=True)
-    widths = (listed_ref.shape[1], mask.shape[1])
-    fan = one_hot(iota(widths, 1) // SUB == iota(widths, 0))
+    fan_shape = (listed_ref.shape[1], mask.shape[1])
+    fan = one_hot(iota(fan_shape, 1) // SUB == iota(fan_shape, 0))
     mask[...] = jnp.dot(
         jnp.broadcast_to(row, listed_ref.shape).astype(BF16), fan, preferred_element_type=F32)
 
@@ -144,31 +145,40 @@
             for p in range(pairs):
                 dst[:, base + p * wide:base + (p + 1) * wide] = gather[pl.ds(p, QB, stride=pairs), :].astype(BF16)
 
-    piece = depth // PIECES
-
-    def to_partner(t):
-        return pltpu.make_async_remote_copy(
-            vis.at[SELF, rows_of(t)], vis.at[PARTNER, rows_of(t)], near_send.at[t], near_recv.at[t],
+    def to_partner(rows):
+        return pltpu.make_async_remote_copy(
+            vis.at[SELF, rows], vis.at[PARTNER, rows], near_send, near_recv,
             device_id=(partner, g), device_id_type=MESH)
 
-    def columns(k):
-        return pl.ds(pl.multiple_of(k * piece, piece), piece)
-
-    def to_cross(t, k):
-        return pltpu.make_async_remote_copy(
-            vis.at[SELF, rows_of(t), columns(k)], vis.at[CROSS, rows_of(t), columns(k)],
-            far_send.at[t, k], far_recv.at[t, k], device_id=(cross, g), device_id_type=MESH)
-
-    def prepare(t, carry):
+    def to_cross(t):
+        return pltpu.make_async_remote_copy(
+            vis.at[SELF, rows_of(t)], vis.at[CROSS, rows_of(t)], far_send, far_recv.at[t],
+            device_id=(cross, g), device_id_type=MESH)
+
+    widths = [depth // fraction for fraction in PIECES]
+    cuts = [slice(sum(widths[:k]), sum(widths[:k + 1])) for k in range(len(widths))]
+
+    def tail_piece(k):
+        at = rows_of(n_chunk - 1), cuts[k]
+        return pltpu.make_async_remote_copy(
+            vis.at[(SELF,) + at], vis.at[(CROSS,) + at], far_send, tail_recv.at[k],
+            device_id=(cross, g), device_id_type=MESH)
+
+    def prepare(i, carry):
+        t = lax.rem(i + 1, n_chunk)
         load_raw(t).wait()
         precondition(raw.at[rows_of(t)], vis.at[SELF, rows_of(t)])
 
-        @pl.when(t > 0)
-        def _():
-            for k in range(PIECES):
-                to_cross(t, k).start()
-
-        to_partner(t).start()
+        @pl.when(jnp.logical_and(t > 0, t < n_chunk - 1))
+        def _():
+            to_cross(t).start()
+
+        @pl.when(t == n_chunk - 1)
+        def _():
+            for k in range(len(cuts)):
+                tail_piece(k).start()
+
+        to_partner(rows_of(t)).start()
         return carry
 
     lax.fori_loop(0, n_chunk, prepare, 0)
@@ -177,17 +187,15 @@
     def to_hop(w, t):
         d, rel, to_x, j = order(t)
         return pltpu.make_async_remote_copy(
-            part.at[w, rows_of(t)], hop.at[w, rel, n_x - 1 - d], hop_send.at[w, t], hop_recv.at[w, rel, n_x - 1 - d],
+            part.at[w, rows_of(t)], hop.at[w, rel, n_x - 1 - d], hop_send.at[w], hop_recv.at[w, rel],
             device_id=(b, yl * n_x + to_x), device_id_type=MESH)
 
+    spans = [slice(at, at + SPAN) for at in range(0, depth, SPAN)]
+
     def score_all(w):
-        part[w] = nt_dot(vis[w, :, 0:piece], slab[:, 0:piece])
-
-        def inner(k, carry):
-            part[w] += nt_dot(vis[w, :, columns(k)], slab[:, columns(k)])
-            return carry
-
-        lax.fori_loop(1, PIECES, inner, 0)
+        for at in spans:
+            product = nt_dot(vis[w, :, at], slab[:, at])
+            part[w] = product if at.start == 0 else part[w] + product
 
         def send(t, carry):
             to_hop(w, t).start()
@@ -195,49 +203,62 @@
 
         lax.fori_loop(0, n_chunk - 2, send, 0)
 
-    def far(t, arrives):
+    def far(t):
         rows = rows_of(t)
-
-        def inner(k, acc):
-            if arrives:
-                to_cross(t, k).wait_recv()
-            return acc + nt_dot(vis[CROSS, rows, columns(k)], slab[:, columns(k)])
-
-        part[CROSS, rows] = lax.fori_loop(0, PIECES, inner, jnp.zeros((QB, part.shape[2]), F32))
+        part[CROSS, rows] = sum(nt_dot(vis[CROSS, rows, at], slab[:, at]) for at in spans)
+
+    def far_pieces(t):
+        rows = rows_of(t)
+        total = 0.0
+        for k, at in enumerate(cuts):
+            tail_piece(k).wait_recv()
+            total += nt_dot(vis[CROSS, rows, at], slab[:, at])
+        part[CROSS, rows] = total
+
+    def far_step(t, carry):
+        @pl.when(t > 0)
+        def _():
+            to_cross(t).wait_recv()
+
+        far(t)
 
         @pl.when(t < n_chunk - 2)
         def _():
             to_hop(CROSS, t).start()
 
-    def far_step(t, carry):
-        far(t, True)
         return carry
 
     owner = (b, partner, cross)
 
     def to_last(w, rel):
         return pltpu.make_async_remote_copy(
-            mine.at[w, rel], last.at[w, rel], last_send.at[w, rel], last_recv.at[w, rel],
+            mine.at[w, rel], last.at[w, rel], last_send.at[min(w, 1)], last_recv.at[w],
             device_id=(owner[w], g if rel == 0 else other), device_id_type=MESH)
 
+    def group(ref, send, recv):
+        return pltpu.make_async_remote_copy(
+            ref, ref, send, recv, device_id=(partner, g), device_id_type=MESH)
+
     def gather_x(w, rel):
-        for d in range(1, n_x):
-            to_hop(w, 2 * (d - 1) + rel).wait_recv()
-        total = part[w, rows_of(n_chunk - 2 + rel)]
+        group(hop.at[w, rel], hop_send.at[w], hop_recv.at[w, rel]).wait_recv()
+        rows = rows_of(n_chunk - 2 + rel)
+        total = part[w, rows]
         for d in range(n_x - 1):
             total = total + hop[w, rel, d]
-        mine[w, rel] = total.astype(mine.dtype)
-        if not (w == SELF and rel == 0):
+        if w == SELF and rel == 0:
+            part[w, rows] = total
+        else:
+            mine[w, rel] = total.astype(mine.dtype)
             to_last(w, rel).start()
 
     def finish(w):
         width = part.shape[2]
-        to_last(w, 1).wait_recv()
         if w == SELF:
-            total = mine[w, 0].astype(F32) + last[w, 1].astype(F32)
+            to_last(w, 1).wait_recv()
+            total = part[w, rows_of(n_chunk - 2)] + last[w, 1].astype(F32)
             o_ref[1] = total * mask[0:1, width:2 * width]
             return
-        to_last(w, 0).wait_recv()
+        group(last.at[w], last_send.at[1], last_recv.at[w]).wait_recv()
         total = last[w, 0].astype(F32) + last[w, 1].astype(F32)
         upper = par == (1 if w == CROSS else 0)
 
@@ -250,8 +271,7 @@
             o_ref[0] = total * mask[0:1, 0:width]
 
     score_all(SELF)
-    for t in range(n_chunk):
-        to_partner(t).wait_recv()
+    to_partner(slice(None)).wait_recv()
     score_all(PARTNER)
 
     for w in (SELF, PARTNER):
@@ -260,37 +280,21 @@
 
     raw_out.wait_recv()
     precondition(vraw, vis.at[CROSS, rows_of(0)])
-    far(0, False)
-    lax.fori_loop(1, n_chunk - 1, far_step, 0)
+    lax.fori_loop(0, n_chunk - 1, far_step, 0)
     gather_x(CROSS, 0)
-    far(n_chunk - 1, True)
+    far_pieces(n_chunk - 1)
     gather_x(CROSS, 1)
     finish(SELF)
     finish(PARTNER)
 
     raw_out.wait_send()
-
-    def drain(t, carry):
-        to_partner(t).wait_send()
-
-        @pl.when(t > 0)
-        def _():
-            for k in range(PIECES):
-                to_cross(t, k).wait_send()
-
-        @pl.when(t < n_chunk - 2)
-        def _():
-            for w in range(3):
-                to_hop(w, t).wait_send()
-
-        return carry
-
-    lax.fori_loop(0, n_chunk, drain, 0)
+    to_partner(slice(None)).wait_send()
+    group(vis.at[SELF, 0:(n_chunk - 1) * QB], far_send, far_recv.at[0]).wait_send()
+    for w in range(3):
+        group(part.at[w, 0:(n_chunk - 2) * QB], hop_send.at[w], hop_recv.at[w, 0]).wait_send()
+    to_last(SELF, 1).wait_send()
+    group(mine.at[1:3], last_send.at[1], last_recv.at[1]).wait_send()
     finish(CROSS)
-    for w in range(3):
-        for rel in range(2):
-            if not (w == SELF and rel == 0):
-                to_last(w, rel).wait_send()
 
 
 def solution(mesh):
@@ -334,14 +338,15 @@
                 dma,
                 dma,
                 dma,
+                dma,
+                dma,
+                dma,
                 dma((n_chunk,)),
-                dma((n_chunk,)),
-                dma((n_chunk, PIECES)),
-                dma((n_chunk, PIECES)),
-                dma((3, n_chunk)),
-                dma((3, 2, n_x - 1)),
+                dma((len(PIECES),)),
+                dma((3,)),
                 dma((3, 2)),
-                dma((3, 2)),
+                dma((2,)),
+                dma((3,)),
             ],
             compiler_params=pltpu.CompilerParams(
                 collective_id=0, has_side_effects=True, vmem_limit_bytes=36 * 2**20),

time: 105 us -> 104 us (level)
  no operation moved by 1% of the time
where the time goes in v4:
time: 104 us
  Pallas kernels  103 us (99%)
    pallas_call x1, Pallas kernels, body(): pl.pallas_call(functools.partial(kernel, n_ex, n_x), out_shape=jax.ShapeD...  103 us

profile of v4, /device:TPU:1, one launch (start us, length us, event | category | flops | bytes accessed | tf_op | source)
XLA Modules:
  0.0 104.2 jit_solution(342962776966278503)
XLA Ops:
  0.0 103.5 %shard_map.55 = f32[3,32,512]{2,1,0:T(8,128)S(1)} custom-call(bf16[256,8192]{1,0:T(8,128)(2,1)} %q_hbm.1, bf16[2,64,64]{2,1,0:T(8,128)(2,1)} %in_hbm.1, bf16[2,64,64]{2,1,0:T(8,128)(2,1)} %out_hbm.1, bf16[512,8192]{1,0:T(8,128)(2,1)} %s_hbm.1, s32[8,24]{1,0:T(8,128)} %listed_hbm.1), custom_call_target="tpu_custom_call" | custom-call | tf_op jit(solution)/shard_map/pallas_call | solution.py:314
  103.5 0.7 copy.7

commit v5 on v4

--- a/solution.py
+++ b/solution.py
@@ -14,7 +14,7 @@
 SUB = 64
 SELF, PARTNER, CROSS = 0, 1, 2
 GROUP = 8
-PIECES = (2, 4, 8, 16, 16)
+PIECES = (4, 4, 4, 8, 16, 16)
 SPAN = 4096
 
 
@@ -209,11 +209,10 @@
 
     def far_pieces(t):
         rows = rows_of(t)
-        total = 0.0
         for k, at in enumerate(cuts):
             tail_piece(k).wait_recv()
-            total += nt_dot(vis[CROSS, rows, at], slab[:, at])
-        part[CROSS, rows] = total
+            product = nt_dot(vis[CROSS, rows, at], slab[:, at])
+            part[CROSS, rows] = product if k == 0 else part[CROSS, rows] + product
 
     def far_step(t, carry):
         @pl.when(t > 0)

time: 104 us -> 103 us (level)
  no operation moved by 1% of the time
where the time goes in v5:
time: 103 us
  Pallas kernels  103 us (100%)
    pallas_call x1, Pallas kernels, body(): pl.pallas_call(functools.partial(kernel, n_ex, n_x), out_shape=jax.ShapeD...  103 us

profile of v5, /device:TPU:1, one launch (start us, length us, event | category | flops | bytes accessed | tf_op | source)
XLA Modules:
  0.0 103.3 jit_solution(7941547595911838186)
XLA Ops:
  0.0 102.6 %shard_map.55 = f32[3,32,512]{2,1,0:T(8,128)S(1)} custom-call(bf16[256,8192]{1,0:T(8,128)(2,1)} %q_hbm.1, bf16[2,64,64]{2,1,0:T(8,128)(2,1)} %in_hbm.1, bf16[2,64,64]{2,1,0:T(8,128)(2,1)} %out_hbm.1, bf16[512,8192]{1,0:T(8,128)(2,1)} %s_hbm.1, s32[8,24]{1,0:T(8,128)} %listed_hbm.1), custom_call_target="tpu_custom_call" | custom-call | tf_op jit(solution)/shard_map/pallas_call | solution.py:313
  102.6 0.7 copy.7

commit v6 on v5

--- a/solution.py
+++ b/solution.py
@@ -273,16 +273,15 @@
     to_partner(slice(None)).wait_recv()
     score_all(PARTNER)
 
-    for w in (SELF, PARTNER):
-        for rel in range(2):
-            gather_x(w, rel)
-
     raw_out.wait_recv()
     precondition(vraw, vis.at[CROSS, rows_of(0)])
     lax.fori_loop(0, n_chunk - 1, far_step, 0)
     gather_x(CROSS, 0)
     far_pieces(n_chunk - 1)
     gather_x(CROSS, 1)
+    for w in (SELF, PARTNER):
+        for rel in range(2):
+            gather_x(w, rel)
     finish(SELF)
     finish(PARTNER)
 

time: 103 us -> 103 us (level)
  no operation moved by 1% of the time
where the time goes in v6:
time: 103 us
  Pallas kernels  103 us (100%)
    pallas_call x1, Pallas kernels, body(): pl.pallas_call(functools.partial(kernel, n_ex, n_x), out_shape=jax.ShapeD...  103 us

profile of v6, /device:TPU:1, one launch (start us, length us, event | category | flops | bytes accessed | tf_op | source)
XLA Modules:
  0.0 103.2 jit_solution(7796250525696943617)
XLA Ops:
  0.0 102.5 %shard_map.55 = f32[3,32,512]{2,1,0:T(8,128)S(1)} custom-call(bf16[256,8192]{1,0:T(8,128)(2,1)} %q_hbm.1, bf16[2,64,64]{2,1,0:T(8,128)(2,1)} %in_hbm.1, bf16[2,64,64]{2,1,0:T(8,128)(2,1)} %out_hbm.1, bf16[512,8192]{1,0:T(8,128)(2,1)} %s_hbm.1, s32[8,24]{1,0:T(8,128)} %listed_hbm.1), custom_call_target="tpu_custom_call" | custom-call | tf_op jit(solution)/shard_map/pallas_call | solution.py:312
  102.6 0.7 copy.7

commit v7 on v6

--- a/solution.py
+++ b/solution.py
@@ -104,7 +104,6 @@
     for i in range(n_chunk):
         load_raw((i + 1) % n_chunk).start()
     slab_copy = pltpu.make_async_copy(s_hbm, slab, slab_sem)
-    slab_copy.start()
 
     pl.semaphore_wait(barrier, len(peers))
 
@@ -112,6 +111,7 @@
         q_hbm.at[rows_of(0)], vraw, vraw_send, vraw_recv,
         device_id=(cross, g), device_id_type=MESH)
     raw_out.start()
+    slab_copy.start()
 
     for copy in small:
         copy.wait()

time: 103 us -> 103 us (level)
  no operation moved by 1% of the time
where the time goes in v7:
time: 103 us
  Pallas kernels  103 us (100%)
    pallas_call x1, Pallas kernels, body(): pl.pallas_call(functools.partial(kernel, n_ex, n_x), out_shape=jax.ShapeD...  103 us

profile of v7, /device:TPU:1, one launch (start us, length us, event | category | flops | bytes accessed | tf_op | source)
XLA Modules:
  0.0 103.2 jit_solution(11182702696100145667)
XLA Ops:
  0.0 102.5 %shard_map.55 = f32[3,32,512]{2,1,0:T(8,128)S(1)} custom-call(bf16[256,8192]{1,0:T(8,128)(2,1)} %q_hbm.1, bf16[2,64,64]{2,1,0:T(8,128)(2,1)} %in_hbm.1, bf16[2,64,64]{2,1,0:T(8,128)(2,1)} %out_hbm.1, bf16[512,8192]{1,0:T(8,128)(2,1)} %s_hbm.1, s32[8,24]{1,0:T(8,128)} %listed_hbm.1), custom_call_target="tpu_custom_call" | custom-call | tf_op jit(solution)/shard_map/pallas_call | solution.py:312
  102.6 0.7 copy.7

commit v8 on v7

--- a/solution.py
+++ b/solution.py
@@ -101,7 +101,7 @@
     ]
     for copy in small:
         copy.start()
-    for i in range(n_chunk):
+    for i in range(2):
         load_raw((i + 1) % n_chunk).start()
     slab_copy = pltpu.make_async_copy(s_hbm, slab, slab_sem)
 
@@ -111,6 +111,8 @@
         q_hbm.at[rows_of(0)], vraw, vraw_send, vraw_recv,
         device_id=(cross, g), device_id_type=MESH)
     raw_out.start()
+    for i in range(2, n_chunk):
+        load_raw((i + 1) % n_chunk).start()
     slab_copy.start()
 
     for copy in small:

time: 103 us -> 103 us (level)
  no operation moved by 1% of the time
where the time goes in v8:
time: 103 us
  Pallas kernels  103 us (100%)
    pallas_call x1, Pallas kernels, body(): pl.pallas_call(functools.partial(kernel, n_ex, n_x), out_shape=jax.ShapeD...  103 us

profile of v8, /device:TPU:1, one launch (start us, length us, event | category | flops | bytes accessed | tf_op | source)
XLA Modules:
  0.0 103.2 jit_solution(15027074088422120151)
XLA Ops:
  0.0 102.5 %shard_map.55 = f32[3,32,512]{2,1,0:T(8,128)S(1)} custom-call(bf16[256,8192]{1,0:T(8,128)(2,1)} %q_hbm.1, bf16[2,64,64]{2,1,0:T(8,128)(2,1)} %in_hbm.1, bf16[2,64,64]{2,1,0:T(8,128)(2,1)} %out_hbm.1, bf16[512,8192]{1,0:T(8,128)(2,1)} %s_hbm.1, s32[8,24]{1,0:T(8,128)} %listed_hbm.1), custom_call_target="tpu_custom_call" | custom-call | tf_op jit(solution)/shard_map/pallas_call | solution.py:314
  102.6 0.7 copy.7
